TPU v7x, 32 devices: a whole 2x2x4 slice. The times are simulated.
32 devices in a mesh: bond: 8 (over z, x), mpo: 4 (over y, core).
Axes of the slice: x: 2, y: 2, z: 4, core: 2. Of those that a mesh axis runs over, the one named last changes fastest.
Arguments:
- wave_blocks: bfloat16 [8, 16, 256, 256], P('bond'), may hold values from -6 to 6
- left_environment: bfloat16 [8, 8, 256, 256], P('mpo', 'bond'), may hold values from -0.375 to 0.375
- right_environment: bfloat16 [8, 8, 256, 256], P('mpo', 'bond'), may hold values from -0.375 to 0.375
- site_operators: bfloat16 [8, 16, 16], P('mpo'), may hold values from -1.1953125 to 1.1953125
- right_sector: int32 [8, 16, 1], P('bond'), may hold values from 0 to 7; in each aligned block of 16 rows (0 to 15, 16 to 31, ..., all dimensions but the last counted through in order) at most 2 rows name the same one
- left_sizes: int32 [8], replicated, may hold values from 128 to 256
- right_sizes: int32 [8], replicated, may hold values from 128 to 256
- sector_place: int32 [8], replicated, may hold values from 0 to 7, each once
Outputs:
- applied: bfloat16 [8, 16, 256, 256], P('bond', 'mpo')
Inputs may be any that keep to these rules, and one draw needn't show every extreme that they name: `right_sector`: among the 16 blocks of one bond index no right sector is named more than 2 times, a bound that some block reaches. `sector_place`: every position is taken by exactly one right sector.
All inputs are finite; a program needn't handle non-finite values.
Results may differ from a plain program's by a relative error of at most 0.0057.
Values may be sent and summed in bfloat16 or wider, within the bound.
A program may use at most 64 MiB of HBM per device.

v0:
```python
import functools

import jax
import jax.numpy as jnp
from jax import lax
from jax.experimental import pallas as pl
from jax.experimental.pallas import tpu as pltpu
from jax.sharding import PartitionSpec as P

MESH = pl.DeviceIdType.MESH


def plane_of(count):
    nx = 1
    while (2 * nx) * (2 * nx) * 2 <= count and count % (2 * nx) == 0:
        nx *= 2
    return count // nx, nx


def kernel(
    n, m,
    sector, place, left_sizes, right_sizes, ops,
    wave_hbm, left_hbm, right_hbm,
    out_ref,
    right_all, wave, left, local_sem, gather_send, gather_recv, *rest,
):
    nz, nx = plane_of(n)
    cores = 2 if m % 2 == 0 else 1
    ny = m // cores
    states, rows, _ = wave.shape
    channels = left.shape[0]
    per = out_ref.shape[0]
    count = ny * per
    pair = ny == 2 and cores == 2
    if pair:
        (part, part_out, part_in, sums,
         part_send, part_recv, sum_send, sum_recv) = rest
    else:
        (mixed, out_core, in_core, out_chip, in_chip, own,
         core_send, core_recv, chip_send, chip_recv) = rest
    b = lax.axis_index("bond")
    p = lax.axis_index("mpo")
    z, x = b // nx, b % nx
    y, c = p // cores, p % cores
    sibling = y * cores + (1 - c)

    wave_copy = pltpu.make_async_copy(wave_hbm, wave, local_sem.at[0])
    left_copy = pltpu.make_async_copy(left_hbm, left, local_sem.at[1])
    own_copy = pltpu.make_async_copy(right_hbm, right_all.at[b], local_sem.at[2])
    wave_copy.start()
    left_copy.start()
    own_copy.start()

    steps = ((nx, z + 1 < nz), (-nx, z > 0), (1, x + 1 < nx), (-1, x > 0))
    barrier = pltpu.get_barrier_semaphore()
    greeted = ny
    for step, there in steps:
        greeted = greeted + there.astype(jnp.int32)

        @pl.when(there)
        def _():
            pl.semaphore_signal(barrier, inc=1, device_id=(b + step, p), device_id_type=MESH)

    pl.semaphore_signal(barrier, inc=1, device_id=(b, sibling), device_id_type=MESH)
    for dy in range(1, ny):
        other = lax.rem(y + dy, ny) * cores + c
        pl.semaphore_signal(barrier, inc=1, device_id=(b, other), device_id_type=MESH)
    pl.semaphore_wait(barrier, greeted)

    def hop(pos, h, k, src):
        return pltpu.make_async_remote_copy(
            src_ref=src,
            dst_ref=right_all.at[pos, h],
            send_sem=gather_send.at[pos, h, k],
            recv_sem=gather_recv.at[pos, h],
            device_id=(b + steps[k][0], p),
            device_id_type=MESH,
        )

    def sends(zs, xs, h):
        column = xs == x
        if nx == 2 and h == channels - 1 and channels > 1:
            detour = (zs == 0) | (zs == nz - 1)
            along, across = column | detour, ~detour | (zs == z)
        else:
            along, across = column, True
        return (
            along & (zs <= z) & (z + 1 < nz),
            along & (zs >= z) & (z > 0),
            across & (xs <= x) & (x + 1 < nx),
            across & (xs >= x) & (x > 0),
        )

    def forward(zs, xs, h):
        pos = zs * nx + xs
        for k, wanted in enumerate(sends(zs, xs, h)):
            @pl.when(wanted)
            def _():
                hop(pos, h, k, right_all.at[pos, h]).start()

    def arrived(pos, h):
        hop(pos, h, 0, right_all.at[pos, h]).wait_recv()

    for h in range(channels):
        for k in (0, 1, 2, 3):
            @pl.when(steps[k][1])
            def _():
                hop(b, h, k, right_hbm.at[h]).start()

    wave_copy.wait()
    left_copy.wait()
    own_copy.wait()

    row_index = lax.broadcasted_iota(jnp.int32, (rows, rows), 0)
    column_index = lax.broadcasted_iota(jnp.int32, (rows, rows), 1)
    live_rows = row_index < left_sizes[b]
    op_row = lax.broadcasted_iota(jnp.int32, (states, states), 0)
    op_column = lax.broadcasted_iota(jnp.int32, (states, states), 1)

    def to_sibling(pos):
        return pltpu.make_async_remote_copy(
            src_ref=part_out.at[pos], dst_ref=part_in.at[pos],
            send_sem=part_send.at[pos], recv_sem=part_recv.at[pos],
            device_id=(b, sibling), device_id_type=MESH,
        )

    def share(kind, pos):
        source, target = (0, 0, 1)[kind], (0, 1, 1)[kind]
        device = (1 - y) * cores + c if kind == 1 else sibling
        return pltpu.make_async_remote_copy(
            src_ref=sums.at[source, pos, c], dst_ref=sums.at[target, pos, c],
            send_sem=sum_send.at[kind, pos], recv_sem=sum_recv.at[target, pos, c],
            device_id=(b, device), device_id_type=MESH,
        )

    def sum_arrived(target, pos, rank):
        pltpu.make_async_remote_copy(
            src_ref=sums.at[target, pos, rank], dst_ref=sums.at[target, pos, rank],
            send_sem=sum_send.at[0, pos], recv_sem=sum_recv.at[target, pos, rank],
            device_id=(b, sibling), device_id_type=MESH,
        ).wait_recv()

    def add_up(pos):
        to_sibling(pos).wait_recv()
        sums[0, pos, c] = (part[pos] + part_in[pos].astype(jnp.float32)).astype(jnp.bfloat16)
        share(1, pos).start()
        share(0, pos).start()

    def pass_on(pos):
        sum_arrived(1, pos, c)
        share(2, pos).start()

    def work(pos):
        def look(s, carry):
            first, last, hits = carry
            hit = place[sector[s]] == pos
            first = jnp.where(hit & (hits == 0), s, first)
            last = jnp.where(hit, s, last)
            return first, last, hits + hit.astype(jnp.int32)

        zero = jnp.int32(0)
        s1, s2, hits = lax.fori_loop(0, states, look, (zero, zero, zero), unroll=True)
        if pair:
            s1, s2 = jnp.where(c == 0, s1, s2), jnp.where(c == 0, s2, s1)
        live = live_rows & (column_index < right_sizes[sector[s1]])

        def masked(s):
            return jnp.where(live, wave[s].astype(jnp.float32), 0.0).astype(jnp.bfloat16)

        both = jnp.concatenate([masked(s1), masked(s2)], axis=0)
        two = hits == 2
        for h in range(channels):
            factor = right_all[pos, h]

            parts = lax.dot_general(
                both, factor, (((1,), (1,)), ((), ())), preferred_element_type=jnp.float32
            ).astype(jnp.bfloat16).astype(jnp.float32)
            p1, p2 = parts[:rows], parts[rows:]
            table = ops[h].astype(jnp.float32)

            def op(s, t, keep=True):
                picked = (op_row == s) & (op_column == t) & keep
                return jnp.sum(jnp.where(picked, table, 0.0), keepdims=True)

            m1 = (op(s1, s1) * p1 + op(s1, s2, two) * p2).astype(jnp.bfloat16)
            m2 = (op(s2, s1, two) * p1 + op(s2, s2) * p2).astype(jnp.bfloat16)
            if pair:
                left_m = left[h]
                q1 = jnp.dot(left_m, m1, preferred_element_type=jnp.float32)
                q2 = jnp.dot(left_m, m2, preferred_element_type=jnp.float32)
                total1, total2 = (q1, q2) if h == 0 else (total1 + q1, total2 + q2)
            else:
                mixed[2 * pos, h] = m1
                mixed[2 * pos + 1, h] = m2
        if pair:
            part_out[pos] = total2.astype(jnp.bfloat16)
            to_sibling(pos).start()
            part[pos] = total1

    def at(g, i, body):
        sign = 1 - 2 * (i % 2)
        e = i // 2
        d = g - (e > 0).astype(jnp.int32)
        zs = z + sign * d
        xs = x + (e + 1) // 2 * (1 - 2 * (e % 2))

        @pl.when((zs >= 0) & (zs < nz) & (xs >= 0) & (xs < nx) & (d >= 0) & ((d > 0) | (sign > 0)))
        def _():
            body(zs, xs)

    items = 2 * (2 * nx - 1)

    def each(g, body):
        def one(i, _):
            at(g, i, body)
            return 0

        lax.fori_loop(0, items, one, 0)

    def multiply(g):
        def one(i, _):
            @pl.when(i < items)
            def _():
                at(g, i, use)

            @pl.when(i >= 2)
            def _():
                at(g, i - 2, lambda zs, xs: add_up(zs * nx + xs))

            return 0

        lax.fori_loop(0, items + 2, one, 0)

    def use(zs, xs):
        pos = zs * nx + xs

        @pl.when(xs != x)
        def _():
            for h in range(channels):
                arrived(pos, h)
                forward(zs, xs, h)

        work(pos)

    def gather_round(g, _):
        @pl.when((g > 0) & (g < nz))
        def _():
            for h in range(channels):
                for sign in (1, -1):
                    zs = z + sign * g

                    @pl.when((zs >= 0) & (zs < nz))
                    def _():
                        arrived(zs * nx + x, h)
                        forward(zs, x, h)

        @pl.when(g <= nz)
        def _():
            if pair:
                multiply(g)
            else:
                each(g, use)

        if pair:
            @pl.when(g > 1)
            def _():
                each(g - 2, lambda zs, xs: pass_on(zs * nx + xs))

        return 0

    lax.fori_loop(0, nz + (3 if pair else 1), gather_round, 0)

    def rank_of(s):
        def look(t, rank):
            return rank + ((t < s) & (sector[t] == sector[s])).astype(jnp.int32)

        return jnp.minimum(lax.fori_loop(0, states, look, jnp.int32(0), unroll=True), 1)

    def finish(pos, _):
        for h in range(channels):
            for k, wanted in enumerate(sends(pos // nx, pos % nx, h)):
                @pl.when(wanted)
                def _():
                    hop(pos, h, k, right_all.at[pos, h]).wait_send()
        if pair:
            to_sibling(pos).wait_send()
            for kind in range(3):
                share(kind, pos).wait_send()
        return 0

    if pair:
        def all_here(pos, _):
            sum_arrived(0, pos, 1 - c)
            sum_arrived(1, pos, 1 - c)
            return 0

        lax.fori_loop(0, n, all_here, 0)
        for q in range(per):
            s = p * per + q
            at, rank = place[sector[s]], rank_of(s)
            total = sums[0, at, rank].astype(jnp.float32) + sums[1, at, rank].astype(jnp.float32)
            live = live_rows & (column_index < right_sizes[sector[s]])
            out_ref[q] = jnp.where(live, total, 0.0).astype(jnp.bfloat16)
        lax.fori_loop(0, n, finish, 0)
        return

    def product(s):
        slot = 2 * place[sector[s]] + rank_of(s)
        total = jnp.dot(left[0], mixed[slot, 0], preferred_element_type=jnp.float32)
        for h in range(1, channels):
            total += jnp.dot(left[h], mixed[slot, h], preferred_element_type=jnp.float32)
        return total

    def owner_chip(i):
        return lax.rem(y + 1 + i // per, ny)

    def to_core(i):
        return pltpu.make_async_remote_copy(
            src_ref=out_core.at[i], dst_ref=in_core.at[i],
            send_sem=core_send.at[i], recv_sem=core_recv.at[i],
            device_id=(b, sibling), device_id_type=MESH,
        )

    def to_chip(i):
        return pltpu.make_async_remote_copy(
            src_ref=out_chip.at[i], dst_ref=in_chip.at[i],
            send_sem=chip_send.at[i], recv_sem=chip_recv.at[i],
            device_id=(b, owner_chip(i) * cores + c), device_id_type=MESH,
        )

    remote = (ny - 1) * per
    lag = min(3, count)

    def reduce_step(i, _):
        @pl.when(i < count)
        def _():
            s = (owner_chip(i) * cores + (1 - c)) * per + i % per
            out_core[i] = product(s).astype(jnp.bfloat16)
            to_core(i).start()

        @pl.when(i >= lag)
        def _():
            j = i - lag
            s = (owner_chip(j) * cores + c) * per + j % per
            total = product(s)
            to_core(j).wait_recv()
            total = total + in_core[j].astype(jnp.float32)

            @pl.when(j < remote)
            def _():
                out_chip[j] = total.astype(jnp.bfloat16)
                to_chip(j).start()

            @pl.when(j >= remote)
            def _():
                own[j - remote] = total

        return 0

    lax.fori_loop(0, count + lag, reduce_step, 0)

    for q in range(per):
        total = own[q]
        for dy in range(ny - 1):
            to_chip(dy * per + q).wait_recv()
            total = total + in_chip[dy * per + q].astype(jnp.float32)
        live = live_rows & (column_index < right_sizes[sector[p * per + q]])
        out_ref[q] = jnp.where(live, total, 0.0).astype(jnp.bfloat16)

    lax.fori_loop(0, n, finish, 0)

    def finish_core(i, _):
        to_core(i).wait_send()
        return 0

    lax.fori_loop(0, count, finish_core, 0)

    def finish_chip(i, _):
        to_chip(i).wait_send()
        return 0

    lax.fori_loop(0, remote, finish_chip, 0)


def shards(n, m, wave_blocks, left_environment, right_environment, site_operators,
           right_sector, left_sizes, right_sizes, sector_place):
    states, rows = wave_blocks.shape[1:3]
    channels = left_environment.shape[0]
    per = states // m
    cores = 2 if m % 2 == 0 else 1
    ny = m // cores
    count = ny * per
    remote = max(1, (ny - 1) * per)
    block = (rows, rows)
    bf16, f32 = jnp.bfloat16, jnp.float32
    smem = pl.BlockSpec(memory_space=pltpu.SMEM)
    hbm = pl.BlockSpec(memory_space=pl.ANY)
    dma = pltpu.SemaphoreType.DMA
    if ny == 2 and cores == 2:
        rest = [
            pltpu.VMEM((n,) + block, f32),
            pltpu.VMEM((n,) + block, bf16),
            pltpu.VMEM((n,) + block, bf16),
            pltpu.VMEM((2, n, 2) + block, bf16),
            dma((n,)), dma((n,)), dma((3, n)), dma((2, n, 2)),
        ]
    else:
        rest = [
            pltpu.VMEM((2 * n, channels) + block, bf16),
            pltpu.VMEM((count,) + block, bf16),
            pltpu.VMEM((count,) + block, bf16),
            pltpu.VMEM((remote,) + block, bf16),
            pltpu.VMEM((remote,) + block, bf16),
            pltpu.VMEM((per,) + block, f32),
            dma((count,)), dma((count,)), dma((remote,)), dma((remote,)),
        ]
    out = pl.pallas_call(
        functools.partial(kernel, n, m),
        out_shape=jax.ShapeDtypeStruct((per,) + block, bf16),
        in_specs=[smem] * 4 + [pl.BlockSpec(memory_space=pltpu.VMEM)] + [hbm] * 3,
        out_specs=pl.BlockSpec(memory_space=pltpu.VMEM),
        scratch_shapes=[
            pltpu.VMEM((n, channels) + block, bf16),
            pltpu.VMEM((states,) + block, bf16),
            pltpu.VMEM((channels,) + block, bf16),
            pltpu.SemaphoreType.DMA((3,)),
            pltpu.SemaphoreType.DMA((n, channels, 4)),
            pltpu.SemaphoreType.DMA((n, channels)),
            *rest,
        ],
        compiler_params=pltpu.CompilerParams(
            collective_id=0, has_side_effects=True, vmem_limit_bytes=60 * 1024 * 1024
        ),
    )(
        right_sector.reshape(states), sector_place, left_sizes, right_sizes,
        site_operators,
        wave_blocks.reshape((states,) + block),
        left_environment.reshape((channels,) + block),
        right_environment.reshape((channels,) + block),
    )
    return out.reshape((1, per) + block)


def solution(mesh):
    placed = (
        P("bond", None, None, None),
        P("mpo", "bond", None, None),
        P("mpo", "bond", None, None),
        P("mpo", None, None),
        P("bond", None, None),
        P(),
        P(),
        P(),
    )
    body = functools.partial(shards, mesh.shape["bond"], mesh.shape["mpo"])
    return jax.shard_map(
        body, mesh=mesh, in_specs=placed, out_specs=P("bond", "mpo", None, None), check_vma=False
    )
```

profile of v0, /device:TPU:0, one launch (start us, length us, event | category | flops | bytes accessed | tf_op | source)
XLA Modules:
  0.0 42.3 jit_solution(14516254111927675252)
XLA Ops:
  0.0 40.4 %shard_map.82 = bf16[4,256,256]{2,1,0:T(8,128)(2,1)} custom-call(s32[16]{0:T(128)} %bitcast.9, s32[8]{0:T(128)} %place.1, s32[8]{0:T(128)} %left_sizes.1, s32[8]{0:T(128)} %right_sizes.1, bf16[2,16,16]{2,1,0:T(8,128)(2,1)} %ops.1, bf16[16,256,256]{2,1,0:T(8,128)(2,1)} %bitcast.5, bf16[2,256,256]{2,1,0:T(8,128)(2,1)} %bitcast.7, bf16[2,256,256]{2,1,0:T(8,128)(2,1)} %bitcast.8), custom_call_target="tpu_custom_call" | custom-call | tf_op jit(solution)/shard_map/pallas_call | solution.py:417
  40.4 1.9 %copy.10 = bf16[1,4,256,256]{3,2,1,0:T(8,128)(2,1)} copy(bf16[1,4,256,256]{3,2,1,0:T(8,128)(2,1)} %bitcast.6) | data formatting | bytes 1048576
where the time goes:
time: 42.7 us; the launch traced here: 42.3 us
  Pallas kernels  40.4 us (95%)
  local copies, waits for them, and re-layouts  1.87 us (4%)
    pallas_call x1, Pallas kernels, shards(): pl.pallas_call(functools.partial(kernel, n, m), out_shape=jax.ShapeDtypeS...  40.4 us
    unnamed x1, local copies, waits for them, and re-layouts  1.87 us

commit v1 on v0

--- a/solution.py
+++ b/solution.py
@@ -382,6 +382,375 @@
     lax.fori_loop(0, remote, finish_chip, 0)
 
 
+def sum_of(k, values):
+    if isinstance(k, int):
+        return values[k]
+    total = 0
+    for i, v in enumerate(values):
+        if v:
+            total = total + (k == i).astype(jnp.int32) * v
+    return total
+
+
+def halves_kernel(
+    n, m,
+    sector, place, left_sizes, right_sizes, ops_ref,
+    wave_hbm, left_hbm, right_hbm,
+    out_ref,
+    right_all, wave, left, ops, coef, part, part_out, part_in, fin, arr, states_of, mine,
+    local_sem, gather_send, gather_recv, first_send, left_send, left_recv, ops_send, ops_recv,
+    part_send, part_recv, fin_send, fin_recv, pass_send, pass_recv,
+):
+    nz, nx = plane_of(n)
+    states, rows, _ = wave.shape
+    half = rows // 2
+    channels = left_hbm.shape[0]
+    per = out_ref.shape[0]
+    units = 2 * channels
+    b = lax.axis_index("bond")
+    p = lax.axis_index("mpo")
+    z, x = b // nx, b % nx
+    y, c = p // 2, p % 2
+    sibling = y * 2 + (1 - c)
+    peer = (1 - y) * 2 + c
+    end = (z == 0) | (z == nz - 1)
+    way = 1 - 2 * (z >= nz // 2).astype(jnp.int32)
+    bf16, f32 = jnp.bfloat16, jnp.float32
+    L, S, X = 0, 1, 2
+    targets = (b + way * nx, b - way * nx, z * nx + (1 - x))
+
+    def own_half(h, of):
+        return right_hbm.at[h, pl.ds(pl.multiple_of(of * half, half), half)]
+
+    wave_copy = pltpu.make_async_copy(wave_hbm, wave, local_sem.at[0])
+    left_copy = pltpu.make_async_copy(left_hbm, left.at[pl.ds(0, channels)], local_sem.at[1])
+    own_copies = [
+        pltpu.make_async_copy(own_half(h, y), right_all.at[b, h], local_sem.at[2 + h])
+        for h in range(channels)
+    ]
+    wave_copy.start()
+    left_copy.start()
+    for own in own_copies:
+        own.start()
+
+    barrier = pltpu.get_barrier_semaphore()
+    for target in (L, X):
+        pl.semaphore_signal(barrier, inc=1, device_id=(targets[target], p), device_id_type=MESH)
+
+    @pl.when(jnp.logical_not(end))
+    def _():
+        pl.semaphore_signal(barrier, inc=1, device_id=(targets[S], p), device_id_type=MESH)
+
+    for other in (sibling, peer):
+        pl.semaphore_signal(barrier, inc=1, device_id=(b, other), device_id_type=MESH)
+    pl.semaphore_wait(barrier, 5 - end.astype(jnp.int32))
+
+    def to_device(src, dst, send, recv, device):
+        return pltpu.make_async_remote_copy(
+            src_ref=src, dst_ref=dst, send_sem=send, recv_sem=recv,
+            device_id=device, device_id_type=MESH,
+        )
+
+    def hop(pos, u, kind, src):
+        return to_device(
+            src, right_all.at[pos, u], gather_send.at[pos, u, kind], gather_recv.at[pos, u],
+            (targets[kind], p),
+        )
+
+    def first(h):
+        return to_device(
+            own_half(h, 1 - y), right_all.at[b, channels + h], first_send.at[h],
+            gather_recv.at[b, channels + h], (b, peer),
+        )
+
+    def left_to_peer(h):
+        return to_device(
+            left_hbm.at[h], left.at[channels + h], left_send.at[h], left_recv.at[h], (b, peer)
+        )
+
+    ops_to_peer = to_device(
+        ops_ref, ops.at[pl.ds(channels, channels)], ops_send, ops_recv, (b, peer)
+    )
+
+    for h in range(channels):
+        first(h).start()
+        for kind in (L, X):
+            hop(b, h, kind, own_half(h, y)).start()
+
+        @pl.when(jnp.logical_not(end))
+        def _():
+            hop(b, h, S, own_half(h, y)).start()
+
+    ops_to_peer.start()
+    for h in range(channels):
+        left_to_peer(h).start()
+
+    def place_of(off, other):
+        return (z + way * off) * nx + ((1 - x) if other else x)
+
+    def event(off, other, u, kinds):
+        pos = place_of(off, other)
+        hop(pos, u, X, right_all.at[pos, u]).wait_recv()
+        for kind in kinds:
+            hop(pos, u, kind, right_all.at[pos, u]).start()
+
+    def sent(off, other, u, kinds):
+        pos = place_of(off, other)
+        for kind in kinds:
+            hop(pos, u, kind, right_all.at[pos, u]).wait_send()
+
+    lo, hi = range(channels), range(channels, units)
+    end_order = [(0, 0), (0, 1), (1, 0), (1, 1), (2, 0), (2, 1), (3, 0), (3, 1)]
+    mid_order = [(0, 0), (0, 1), (-1, 0), (1, 0), (-1, 1), (2, 0), (1, 1), (2, 1)]
+    end_before = {
+        "start": [(0, 0, 2, (L, X)), (1, 0, 0, (X,)), (0, 0, 3, (L, X))]
+        + [(1, 0, u, (X,)) for u in (1, 2, 3)]
+        + [(0, 1, u, ()) for u in lo] + [(0, 1, u, (L,)) for u in hi] + [(2, 0, 0, (X,))],
+        1: [(2, 0, 1, (X,))],
+        2: [(2, 0, 2, (X,))],
+        3: [(2, 0, 3, (X,))] + [(1, 1, u, ()) for u in range(units)],
+        5: [(3, 0, u, (X,)) for u in lo] + [(2, 1, u, ()) for u in range(units)],
+        6: [(3, 0, u, ()) for u in hi],
+        7: [(3, 1, u, ()) for u in range(units)],
+    }
+    mid_before = {
+        "start": [
+            (0, 0, 2, (L, S, X)), (-1, 0, 0, (L, X)), (1, 0, 0, (S, X)),
+            (0, 0, 3, (L, S, X)), (-1, 0, 1, (L, X)), (1, 0, 1, (S, X)),
+            (-1, 0, 2, (L,)), (1, 0, 2, (S, X)), (-1, 0, 3, (L,)), (1, 0, 3, (S, X)),
+        ] + [(0, 1, u, ()) for u in range(units)] + [(2, 0, 0, (S, X)), (-1, 1, 2, (L,))],
+        1: [(2, 0, 1, (S, X)), (-1, 1, 3, (L,))],
+        2: [(2, 0, 2, (S,))],
+        3: [(2, 0, 3, (S,))],
+        4: [(-1, 1, u, ()) for u in lo],
+        6: [(2, 1, u, (S,)) for u in hi] + [(1, 1, u, ()) for u in range(units)],
+        7: [(2, 1, u, ()) for u in lo],
+    }
+
+    def run(stage):
+        @pl.when(end)
+        def _():
+            for e in end_before.get(stage, ()):
+                event(*e)
+
+        @pl.when(jnp.logical_not(end))
+        def _():
+            for e in mid_before.get(stage, ()):
+                event(*e)
+
+    def pos_of(k):
+        off = jnp.where(end, sum_of(k, [o for o, _ in end_order]), sum_of(k, [o for o, _ in mid_order]))
+        other = jnp.where(end, sum_of(k, [o for _, o in end_order]), sum_of(k, [o for _, o in mid_order]))
+        return (z + way * off) * nx + x + other * (1 - 2 * x)
+
+    def list_states(k, _):
+        pos = pos_of(k)
+
+        def look(s, carry):
+            s1, s2 = carry
+            hit = place[sector[s]] == pos
+            return jnp.where(hit & (s < s1), s, s1), jnp.where(hit, s, s2)
+
+        s1, s2 = lax.fori_loop(0, states, look, (jnp.int32(states - 1), jnp.int32(0)), unroll=True)
+        states_of[k, 0] = s1
+        states_of[k, 1] = s2
+        states_of[k, 2] = right_sizes[sector[s1]]
+        return 0
+
+    lax.fori_loop(0, n, list_states, 0)
+
+    def list_mine(q, _):
+        s = p * per + q
+
+        def look(t, rank):
+            return rank + ((t < s) & (sector[t] == sector[s])).astype(jnp.int32)
+
+        mine[q, 0] = place[sector[s]]
+        mine[q, 1] = jnp.minimum(lax.fori_loop(0, states, look, jnp.int32(0), unroll=True), 1)
+        return 0
+
+    lax.fori_loop(0, per, list_mine, 0)
+
+    ops[pl.ds(0, channels)] = ops_ref[...]
+    run("start")
+
+    ops_to_peer.wait_recv()
+    square = (states, states)
+    op_row = lax.broadcasted_iota(jnp.int32, square, 0)
+    op_column = lax.broadcasted_iota(jnp.int32, square, 1)
+    named = jnp.zeros(square, jnp.int32)
+    for r in range(states):
+        named = jnp.where(op_row == r, states_of[r // 2, r % 2], named)
+    pick = jnp.where(named == op_column, 1.0, 0.0).astype(bf16)
+    same = op_row == op_column
+    twin = op_row + 1 - 2 * (op_row % 2) == op_column
+    for u in range(units):
+        picked = jnp.dot(pick, ops[u], preferred_element_type=f32).astype(bf16)
+        table = lax.dot_general(
+            picked, pick, (((1,), (1,)), ((), ())), preferred_element_type=f32
+        )
+        for i, chosen in enumerate((same, twin)):
+            column = jnp.sum(jnp.where(chosen, table, 0.0), axis=1, keepdims=True)
+            coef[u, i] = jnp.broadcast_to(column, (states, 128))
+
+    wave_copy.wait()
+    left_copy.wait()
+    for own in own_copies:
+        own.wait()
+    for h in range(channels):
+        left_to_peer(h).wait_recv()
+
+    row_index = lax.broadcasted_iota(jnp.int32, (rows, rows), 0)
+    column_index = lax.broadcasted_iota(jnp.int32, (rows, rows), 1)
+    half_row = lax.broadcasted_iota(jnp.int32, (rows, half), 0)
+    half_column = lax.broadcasted_iota(jnp.int32, (rows, half), 1) + y * half
+
+    def to_sibling(pos):
+        return to_device(
+            part_out.at[pos], part_in.at[pos], part_send.at[pos], part_recv.at[pos], (b, sibling)
+        )
+
+    def to_peer(pos):
+        return to_device(
+            fin.at[pos, c], arr.at[pos, c], fin_send.at[pos], fin_recv.at[pos], (b, peer)
+        )
+
+    def passing(pos, rank):
+        return to_device(
+            arr.at[pos, rank], arr.at[pos, rank], pass_send.at[pos], pass_recv.at[pos], (b, sibling)
+        )
+
+    def compute(k):
+        pos = pos_of(k)
+        s1, s2 = states_of[k, 0], states_of[k, 1]
+        live = (row_index < left_sizes[b]) & (column_index < states_of[k, 2])
+
+        def masked(s):
+            return jnp.where(live, wave[s].astype(f32), 0.0).astype(bf16)
+
+        both = jnp.concatenate([masked(s1), masked(s2)], axis=0)
+        total = None
+        for g in range(2):
+            factor = right_all[pos, pl.ds(g * channels, channels)].reshape(channels * half, rows)
+            parts = lax.dot_general(
+                both, factor, (((1,), (1,)), ((), ())), preferred_element_type=f32
+            ).astype(bf16).astype(f32)
+            for h in range(channels):
+                u = g * channels + h
+                p1 = parts[:rows, h * half:(h + 1) * half]
+                p2 = parts[rows:, h * half:(h + 1) * half]
+                own1, own2 = coef[u, 0, pl.ds(2 * k, 1)], coef[u, 0, pl.ds(2 * k + 1, 1)]
+                cross1, cross2 = coef[u, 1, pl.ds(2 * k, 1)], coef[u, 1, pl.ds(2 * k + 1, 1)]
+                mixed = jnp.concatenate(
+                    [(own1 * p1 + cross1 * p2).astype(bf16), (cross2 * p1 + own2 * p2).astype(bf16)],
+                    axis=1,
+                )
+                product = jnp.dot(left[u], mixed, preferred_element_type=f32)
+                total = product if total is None else total + product
+        part_out[pos] = total.astype(bf16)
+        to_sibling(pos).start()
+        part[pos] = total
+
+    def add_up(k):
+        pos = pos_of(k)
+        to_sibling(pos).wait_recv()
+        live = (half_row < left_sizes[b]) & (half_column < states_of[k, 2])
+        for r in range(2):
+            cut = slice(r * half, (r + 1) * half)
+            total = part[pos, :, cut] + part_in[pos, :, cut].astype(f32)
+            fin[pos, r] = jnp.where(live, total, 0.0).astype(bf16)
+        to_peer(pos).start()
+
+    def pass_on(k):
+        pos = pos_of(k)
+        to_peer(pos).wait_recv()
+        passing(pos, c).start()
+
+    def step(k, _):
+        @pl.when(k >= 5)
+        def _():
+            add_up(k - 1)
+
+        @pl.when(k == 7)
+        def _():
+            pass_on(4)
+            pass_on(5)
+
+            @pl.when(end)
+            def _():
+                for h in lo:
+                    sent(0, 0, h, (L, X))
+                for events in end_before.values():
+                    for e in events:
+                        sent(*e)
+
+            @pl.when(jnp.logical_not(end))
+            def _():
+                for h in lo:
+                    sent(0, 0, h, (L, S, X))
+                for stage, events in mid_before.items():
+                    for e in events:
+                        if stage != 6:
+                            sent(*e)
+
+        for stage in range(1, n):
+            if stage in end_before or stage in mid_before:
+                @pl.when(k == stage)
+                def _():
+                    run(stage)
+
+        compute(k)
+
+        @pl.when((k >= 1) & (k < 5))
+        def _():
+            add_up(k - 1)
+
+        @pl.when((k >= 3) & (k < 7))
+        def _():
+            pass_on(k - 3)
+
+        return 0
+
+    lax.fori_loop(0, n, step, 0)
+    pass_on(6)
+    add_up(7)
+    for h in range(channels):
+        first(h).wait_send()
+        left_to_peer(h).wait_send()
+    ops_to_peer.wait_send()
+
+    @pl.when(jnp.logical_not(end))
+    def _():
+        for e in mid_before[6]:
+            sent(*e)
+
+    def settle(pos, _):
+        to_sibling(pos).wait_send()
+        to_peer(pos).wait_send()
+        return 0
+
+    lax.fori_loop(0, n, settle, 0)
+    pass_on(7)
+
+    def all_here(pos, _):
+        passing(pos, 1 - c).wait_recv()
+        return 0
+
+    lax.fori_loop(0, n, all_here, 0)
+    mine_at = pl.ds(pl.multiple_of(y * half, half), half)
+    others_at = pl.ds(pl.multiple_of((1 - y) * half, half), half)
+    for q in range(per):
+        pos, rank = mine[q, 0], mine[q, 1]
+        out_ref[q, :, mine_at] = fin[pos, rank]
+        out_ref[q, :, others_at] = arr[pos, rank]
+
+    def let_go(pos, _):
+        passing(pos, c).wait_send()
+        return 0
+
+    lax.fori_loop(0, n, let_go, 0)
+
+
 def shards(n, m, wave_blocks, left_environment, right_environment, site_operators,
            right_sector, left_sizes, right_sizes, sector_place):
     states, rows = wave_blocks.shape[1:3]
@@ -396,7 +765,30 @@
     smem = pl.BlockSpec(memory_space=pltpu.SMEM)
     hbm = pl.BlockSpec(memory_space=pl.ANY)
     dma = pltpu.SemaphoreType.DMA
-    if ny == 2 and cores == 2:
+    nz, nx = plane_of(n)
+    by_halves = (nz, nx, ny, cores, channels) == (4, 2, 2, 2, 2) and states == 2 * n
+    if by_halves:
+        half = (rows // 2, rows)
+        tall = (rows, rows // 2)
+        scratch = [
+            pltpu.VMEM((n, 2 * channels) + half, bf16),
+            pltpu.VMEM((states,) + block, bf16),
+            pltpu.VMEM((2 * channels,) + block, bf16),
+            pltpu.VMEM((2 * channels, states, states), bf16),
+            pltpu.VMEM((2 * channels, 2, states, 128), f32),
+            pltpu.VMEM((n,) + block, f32),
+            pltpu.VMEM((n,) + block, bf16),
+            pltpu.VMEM((n,) + block, bf16),
+            pltpu.VMEM((n, 2) + tall, bf16),
+            pltpu.VMEM((n, 2) + tall, bf16),
+            pltpu.SMEM((n, 3), jnp.int32),
+            pltpu.SMEM((per, 2), jnp.int32),
+            dma((2 + channels,)),
+            dma((n, 2 * channels, 3)), dma((n, 2 * channels)),
+            dma((channels,)), dma((channels,)), dma((channels,)), dma, dma,
+            dma((n,)), dma((n,)), dma((n,)), dma((n,)), dma((n,)), dma((n,)),
+        ]
+    elif ny == 2 and cores == 2:
         rest = [
             pltpu.VMEM((n,) + block, f32),
             pltpu.VMEM((n,) + block, bf16),
@@ -414,20 +806,20 @@
             pltpu.VMEM((per,) + block, f32),
             dma((count,)), dma((count,)), dma((remote,)), dma((remote,)),
         ]
+    if not by_halves:
+        scratch = [
+            pltpu.VMEM((n, channels) + block, bf16),
+            pltpu.VMEM((states,) + block, bf16),
+            pltpu.VMEM((channels,) + block, bf16),
+            dma((3,)), dma((n, channels, 4)), dma((n, channels)),
+            *rest,
+        ]
     out = pl.pallas_call(
-        functools.partial(kernel, n, m),
+        functools.partial(halves_kernel if by_halves else kernel, n, m),
         out_shape=jax.ShapeDtypeStruct((per,) + block, bf16),
         in_specs=[smem] * 4 + [pl.BlockSpec(memory_space=pltpu.VMEM)] + [hbm] * 3,
         out_specs=pl.BlockSpec(memory_space=pltpu.VMEM),
-        scratch_shapes=[
-            pltpu.VMEM((n, channels) + block, bf16),
-            pltpu.VMEM((states,) + block, bf16),
-            pltpu.VMEM((channels,) + block, bf16),
-            pltpu.SemaphoreType.DMA((3,)),
-            pltpu.SemaphoreType.DMA((n, channels, 4)),
-            pltpu.SemaphoreType.DMA((n, channels)),
-            *rest,
-        ],
+        scratch_shapes=scratch,
         compiler_params=pltpu.CompilerParams(
             collective_id=0, has_side_effects=True, vmem_limit_bytes=60 * 1024 * 1024
         ),

time: 42.7 us -> 43.8 us (1.026)
  Pallas kernels: 40.4 us -> 41.7 us
    pallas_call x1, Pallas kernels: 40.4 us -> 41.7 us  [shards(): pl.pallas_call(functools.partial(halves_kernel if by_halves else kernel,...]
where the time goes in v1:
time: 43.8 us; the launch traced here: 43.6 us
  Pallas kernels  41.7 us (95%)
  local copies, waits for them, and re-layouts  1.87 us (4%)
    pallas_call x1, Pallas kernels, shards(): pl.pallas_call(functools.partial(halves_kernel if by_halves else kernel,...  41.7 us
    unnamed x1, local copies, waits for them, and re-layouts  1.87 us

profile of v1, /device:TPU:0, one launch (start us, length us, event | category | flops | bytes accessed | tf_op | source)
XLA Modules:
  0.0 43.6 jit_solution(3954472228959554110)
XLA Ops:
  0.0 41.7 %shard_map.82 = bf16[4,256,256]{2,1,0:T(8,128)(2,1)} custom-call(s32[16]{0:T(128)} %bitcast.9, s32[8]{0:T(128)} %place.1, s32[8]{0:T(128)} %left_sizes.1, s32[8]{0:T(128)} %right_sizes.1, bf16[2,16,16]{2,1,0:T(8,128)(2,1)} %ops_ref.1, bf16[16,256,256]{2,1,0:T(8,128)(2,1)} %bitcast.5, bf16[2,256,256]{2,1,0:T(8,128)(2,1)} %bitcast.7, bf16[2,256,256]{2,1,0:T(8,128)(2,1)} %bitcast.8), custom_call_target="tpu_custom_call" | custom-call | tf_op jit(solution)/shard_map/pallas_call | solution.py:817
  41.7 1.9 %copy.10 = bf16[1,4,256,256]{3,2,1,0:T(8,128)(2,1)} copy(bf16[1,4,256,256]{3,2,1,0:T(8,128)(2,1)} %bitcast.6) | data formatting | bytes 1048576

commit v2 on v1

--- a/solution.py
+++ b/solution.py
@@ -397,8 +397,8 @@
     sector, place, left_sizes, right_sizes, ops_ref,
     wave_hbm, left_hbm, right_hbm,
     out_ref,
-    right_all, wave, left, ops, coef, part, part_out, part_in, fin, arr, states_of, mine,
-    local_sem, gather_send, gather_recv, first_send, left_send, left_recv, ops_send, ops_recv,
+    right_all, away, wave, left, ops, coef, part, part_out, part_in, fin, arr, states_of, mine,
+    local_sem, gather_send, gather_recv, early_send, left_recv, ops_send, ops_recv,
     part_send, part_recv, fin_send, fin_recv, pass_send, pass_recv,
 ):
     nz, nx = plane_of(n)
@@ -425,13 +425,16 @@
     wave_copy = pltpu.make_async_copy(wave_hbm, wave, local_sem.at[0])
     left_copy = pltpu.make_async_copy(left_hbm, left.at[pl.ds(0, channels)], local_sem.at[1])
     own_copies = [
-        pltpu.make_async_copy(own_half(h, y), right_all.at[b, h], local_sem.at[2 + h])
+        pltpu.make_async_copy(own_half(h, 1 - y), away.at[h], local_sem.at[2])
+        for h in range(channels)
+    ] + [
+        pltpu.make_async_copy(own_half(h, y), right_all.at[b, h], local_sem.at[2])
         for h in range(channels)
     ]
-    wave_copy.start()
-    left_copy.start()
     for own in own_copies:
         own.start()
+    left_copy.start()
+    wave_copy.start()
 
     barrier = pltpu.get_barrier_semaphore()
     for target in (L, X):
@@ -451,36 +454,38 @@
             device_id=device, device_id_type=MESH,
         )
 
-    def hop(pos, u, kind, src):
+    def hop(pos, u, kind, src, batch=1):
         return to_device(
-            src, right_all.at[pos, u], gather_send.at[pos, u, kind], gather_recv.at[pos, u],
+            src, right_all.at[pos, u], gather_send.at[batch], gather_recv.at[pos, u],
             (targets[kind], p),
         )
 
     def first(h):
         return to_device(
-            own_half(h, 1 - y), right_all.at[b, channels + h], first_send.at[h],
+            away.at[h], right_all.at[b, channels + h], early_send,
             gather_recv.at[b, channels + h], (b, peer),
         )
 
     def left_to_peer(h):
         return to_device(
-            left_hbm.at[h], left.at[channels + h], left_send.at[h], left_recv.at[h], (b, peer)
+            left.at[h], left.at[channels + h], early_send, left_recv, (b, peer)
         )
 
     ops_to_peer = to_device(
         ops_ref, ops.at[pl.ds(channels, channels)], ops_send, ops_recv, (b, peer)
     )
 
+    pltpu.make_async_copy(right_hbm, left.at[pl.ds(0, channels)], local_sem.at[2]).wait()
     for h in range(channels):
         first(h).start()
         for kind in (L, X):
-            hop(b, h, kind, own_half(h, y)).start()
+            hop(b, h, kind, right_all.at[b, h], 0).start()
 
         @pl.when(jnp.logical_not(end))
         def _():
-            hop(b, h, S, own_half(h, y)).start()
-
+            hop(b, h, S, right_all.at[b, h], 0).start()
+
+    left_copy.wait()
     ops_to_peer.start()
     for h in range(channels):
         left_to_peer(h).start()
@@ -492,38 +497,41 @@
         pos = place_of(off, other)
         hop(pos, u, X, right_all.at[pos, u]).wait_recv()
         for kind in kinds:
-            hop(pos, u, kind, right_all.at[pos, u]).start()
-
-    def sent(off, other, u, kinds):
-        pos = place_of(off, other)
-        for kind in kinds:
-            hop(pos, u, kind, right_all.at[pos, u]).wait_send()
+            hop(pos, u, kind, right_all.at[pos, u], 0 if (off, other) == (0, 0) else 1).start()
+
+    def settled(view, sem):
+        to_device(view, view, sem, sem, (b, sibling)).wait_send()
 
     lo, hi = range(channels), range(channels, units)
     end_order = [(0, 0), (0, 1), (1, 0), (1, 1), (2, 0), (2, 1), (3, 0), (3, 1)]
     mid_order = [(0, 0), (0, 1), (-1, 0), (1, 0), (-1, 1), (2, 0), (1, 1), (2, 1)]
     end_before = {
-        "start": [(0, 0, 2, (L, X)), (1, 0, 0, (X,)), (0, 0, 3, (L, X))]
-        + [(1, 0, u, (X,)) for u in (1, 2, 3)]
+        "own": [(0, 0, 2, (L, X)), (1, 0, 0, (X,)), (0, 0, 3, (L, X)), (1, 0, 1, (X,))],
+        "start": [(1, 0, u, (X,)) for u in hi]
         + [(0, 1, u, ()) for u in lo] + [(0, 1, u, (L,)) for u in hi] + [(2, 0, 0, (X,))],
         1: [(2, 0, 1, (X,))],
         2: [(2, 0, 2, (X,))],
         3: [(2, 0, 3, (X,))] + [(1, 1, u, ()) for u in range(units)],
-        5: [(3, 0, u, (X,)) for u in lo] + [(2, 1, u, ()) for u in range(units)],
+        4: [(3, 0, 0, (X,))],
+        5: [(3, 0, 1, (X,))],
+        "5+": [(2, 1, u, ()) for u in range(units)],
         6: [(3, 0, u, ()) for u in hi],
         7: [(3, 1, u, ()) for u in range(units)],
     }
     mid_before = {
+        "own": [
+            (0, 0, 2, (L, S, X)), (0, 0, 3, (L, S, X)),
+            (-1, 0, 0, (L, X)), (1, 0, 0, (S, X)), (-1, 0, 1, (L, X)), (1, 0, 1, (S, X)),
+        ],
         "start": [
-            (0, 0, 2, (L, S, X)), (-1, 0, 0, (L, X)), (1, 0, 0, (S, X)),
-            (0, 0, 3, (L, S, X)), (-1, 0, 1, (L, X)), (1, 0, 1, (S, X)),
             (-1, 0, 2, (L,)), (1, 0, 2, (S, X)), (-1, 0, 3, (L,)), (1, 0, 3, (S, X)),
-        ] + [(0, 1, u, ()) for u in range(units)] + [(2, 0, 0, (S, X)), (-1, 1, 2, (L,))],
-        1: [(2, 0, 1, (S, X)), (-1, 1, 3, (L,))],
-        2: [(2, 0, 2, (S,))],
+        ] + [(0, 1, u, ()) for u in range(units)] + [(2, 0, 0, (S, X))],
+        1: [(2, 0, 1, (S, X)), (-1, 1, 2, (L,))],
+        2: [(-1, 1, 3, (L,)), (2, 0, 2, (S,))],
         3: [(2, 0, 3, (S,))],
-        4: [(-1, 1, u, ()) for u in lo],
-        6: [(2, 1, u, (S,)) for u in hi] + [(1, 1, u, ()) for u in range(units)],
+        4: [(2, 1, 2, (S,))] + [(-1, 1, u, ()) for u in lo],
+        5: [(2, 1, 3, (S,))],
+        6: [(1, 1, u, ()) for u in range(units)],
         7: [(2, 1, u, ()) for u in lo],
     }
 
@@ -571,34 +579,34 @@
 
     lax.fori_loop(0, per, list_mine, 0)
 
+    def pick_operators():
+        ops_to_peer.wait_recv()
+        square = (states, states)
+        op_row = lax.broadcasted_iota(jnp.int32, square, 0)
+        op_column = lax.broadcasted_iota(jnp.int32, square, 1)
+        named = jnp.zeros(square, jnp.int32)
+        for r in range(states):
+            named = jnp.where(op_row == r, states_of[r // 2, r % 2], named)
+        pick = jnp.where(named == op_column, 1.0, 0.0).astype(bf16)
+        same = op_row == op_column
+        twin = op_row + 1 - 2 * (op_row % 2) == op_column
+        for u in range(units):
+            picked = jnp.dot(pick, ops[u], preferred_element_type=f32).astype(bf16)
+            table = lax.dot_general(
+                picked, pick, (((1,), (1,)), ((), ())), preferred_element_type=f32
+            )
+            for i, chosen in enumerate((same, twin)):
+                column = jnp.sum(jnp.where(chosen, table, 0.0), axis=1, keepdims=True)
+                coef[u, i] = jnp.broadcast_to(column, (states, 128))
+
     ops[pl.ds(0, channels)] = ops_ref[...]
+    run("own")
+    pick_operators()
     run("start")
 
-    ops_to_peer.wait_recv()
-    square = (states, states)
-    op_row = lax.broadcasted_iota(jnp.int32, square, 0)
-    op_column = lax.broadcasted_iota(jnp.int32, square, 1)
-    named = jnp.zeros(square, jnp.int32)
-    for r in range(states):
-        named = jnp.where(op_row == r, states_of[r // 2, r % 2], named)
-    pick = jnp.where(named == op_column, 1.0, 0.0).astype(bf16)
-    same = op_row == op_column
-    twin = op_row + 1 - 2 * (op_row % 2) == op_column
-    for u in range(units):
-        picked = jnp.dot(pick, ops[u], preferred_element_type=f32).astype(bf16)
-        table = lax.dot_general(
-            picked, pick, (((1,), (1,)), ((), ())), preferred_element_type=f32
-        )
-        for i, chosen in enumerate((same, twin)):
-            column = jnp.sum(jnp.where(chosen, table, 0.0), axis=1, keepdims=True)
-            coef[u, i] = jnp.broadcast_to(column, (states, 128))
-
     wave_copy.wait()
-    left_copy.wait()
-    for own in own_copies:
-        own.wait()
-    for h in range(channels):
-        left_to_peer(h).wait_recv()
+    both_left = left.at[pl.ds(channels, channels)]
+    to_device(both_left, both_left, early_send, left_recv, (b, peer)).wait_recv()
 
     row_index = lax.broadcasted_iota(jnp.int32, (rows, rows), 0)
     column_index = lax.broadcasted_iota(jnp.int32, (rows, rows), 1)
@@ -607,17 +615,17 @@
 
     def to_sibling(pos):
         return to_device(
-            part_out.at[pos], part_in.at[pos], part_send.at[pos], part_recv.at[pos], (b, sibling)
+            part_out.at[pos], part_in.at[pos], part_send, part_recv.at[pos], (b, sibling)
         )
 
     def to_peer(pos):
         return to_device(
-            fin.at[pos, c], arr.at[pos, c], fin_send.at[pos], fin_recv.at[pos], (b, peer)
+            fin.at[pos, c], arr.at[pos, c], fin_send, fin_recv.at[pos], (b, peer)
         )
 
     def passing(pos, rank):
         return to_device(
-            arr.at[pos, rank], arr.at[pos, rank], pass_send.at[pos], pass_recv.at[pos], (b, sibling)
+            arr.at[pos, rank], arr.at[pos, rank], pass_send, pass_recv, (b, sibling)
         )
 
     def compute(k):
@@ -666,77 +674,60 @@
         to_peer(pos).wait_recv()
         passing(pos, c).start()
 
+    def free_sends():
+        settled(left.at[pl.ds(0, channels + channels // 2)], early_send)
+        ops_to_peer.wait_send()
+
+        @pl.when(end)
+        def _():
+            settled(right_all.at[pl.ds(0, 2)], gather_send.at[0])
+            settled(right_all.at[pl.ds(0, 3)], gather_send.at[1])
+
+        @pl.when(jnp.logical_not(end))
+        def _():
+            settled(right_all.at[pl.ds(0, 3)], gather_send.at[0])
+
     def step(k, _):
-        @pl.when(k >= 5)
+        for stage in range(1, n):
+            @pl.when(k == stage)
+            def _():
+                if stage == 7:
+                    add_up(6)
+                    pass_on(3)
+                    pass_on(4)
+                    free_sends()
+                run(stage)
+                if stage == 5:
+                    add_up(4)
+                    pass_on(1)
+                    run("5+")
+
+        compute(k)
+
+        @pl.when((k >= 1) & (k != 5) & (k != 7))
         def _():
             add_up(k - 1)
 
-        @pl.when(k == 7)
-        def _():
-            pass_on(4)
-            pass_on(5)
-
-            @pl.when(end)
-            def _():
-                for h in lo:
-                    sent(0, 0, h, (L, X))
-                for events in end_before.values():
-                    for e in events:
-                        sent(*e)
-
-            @pl.when(jnp.logical_not(end))
-            def _():
-                for h in lo:
-                    sent(0, 0, h, (L, S, X))
-                for stage, events in mid_before.items():
-                    for e in events:
-                        if stage != 6:
-                            sent(*e)
-
-        for stage in range(1, n):
-            if stage in end_before or stage in mid_before:
-                @pl.when(k == stage)
-                def _():
-                    run(stage)
-
-        compute(k)
-
-        @pl.when((k >= 1) & (k < 5))
-        def _():
-            add_up(k - 1)
-
-        @pl.when((k >= 3) & (k < 7))
-        def _():
-            pass_on(k - 3)
+        @pl.when((k == 4) | (k == 6))
+        def _():
+            pass_on(k - 4)
 
         return 0
 
     lax.fori_loop(0, n, step, 0)
+    add_up(7)
+    pass_on(5)
     pass_on(6)
-    add_up(7)
-    for h in range(channels):
-        first(h).wait_send()
-        left_to_peer(h).wait_send()
-    ops_to_peer.wait_send()
 
     @pl.when(jnp.logical_not(end))
     def _():
-        for e in mid_before[6]:
-            sent(*e)
-
-    def settle(pos, _):
-        to_sibling(pos).wait_send()
-        to_peer(pos).wait_send()
-        return 0
-
-    lax.fori_loop(0, n, settle, 0)
+        settled(right_all.at[pl.ds(0, 6)], gather_send.at[1])
+
+    settled(part_out, part_send)
+    settled(arr.at[pl.ds(0, n // 2)], fin_send)
     pass_on(7)
-
-    def all_here(pos, _):
-        passing(pos, 1 - c).wait_recv()
-        return 0
-
-    lax.fori_loop(0, n, all_here, 0)
+    passed = arr.at[pl.ds(0, n // 2)]
+    to_device(passed, passed, pass_send, pass_recv, (b, sibling)).wait_recv()
     mine_at = pl.ds(pl.multiple_of(y * half, half), half)
     others_at = pl.ds(pl.multiple_of((1 - y) * half, half), half)
     for q in range(per):
@@ -744,11 +735,7 @@
         out_ref[q, :, mine_at] = fin[pos, rank]
         out_ref[q, :, others_at] = arr[pos, rank]
 
-    def let_go(pos, _):
-        passing(pos, c).wait_send()
-        return 0
-
-    lax.fori_loop(0, n, let_go, 0)
+    settled(arr.at[pl.ds(0, n // 2)], pass_send)
 
 
 def shards(n, m, wave_blocks, left_environment, right_environment, site_operators,
@@ -772,6 +759,7 @@
         tall = (rows, rows // 2)
         scratch = [
             pltpu.VMEM((n, 2 * channels) + half, bf16),
+            pltpu.VMEM((channels,) + half, bf16),
             pltpu.VMEM((states,) + block, bf16),
             pltpu.VMEM((2 * channels,) + block, bf16),
             pltpu.VMEM((2 * channels, states, states), bf16),
@@ -783,10 +771,8 @@
             pltpu.VMEM((n, 2) + tall, bf16),
             pltpu.SMEM((n, 3), jnp.int32),
             pltpu.SMEM((per, 2), jnp.int32),
-            dma((2 + channels,)),
-            dma((n, 2 * channels, 3)), dma((n, 2 * channels)),
-            dma((channels,)), dma((channels,)), dma((channels,)), dma, dma,
-            dma((n,)), dma((n,)), dma((n,)), dma((n,)), dma((n,)), dma((n,)),
+            dma((3,)), dma((2,)), dma((n, 2 * channels)), dma, dma, dma, dma,
+            dma, dma((n,)), dma, dma((n,)), dma, dma,
         ]
     elif ny == 2 and cores == 2:
         rest = [
@@ -816,7 +802,7 @@
         ]
     out = pl.pallas_call(
         functools.partial(halves_kernel if by_halves else kernel, n, m),
-        out_shape=jax.ShapeDtypeStruct((per,) + block, bf16),
+        out_shape=pltpu.VMEM((per,) + block, bf16),
         in_specs=[smem] * 4 + [pl.BlockSpec(memory_space=pltpu.VMEM)] + [hbm] * 3,
         out_specs=pl.BlockSpec(memory_space=pltpu.VMEM),
         scratch_shapes=scratch,

time: 43.8 us -> 34.6 us (0.79)
  Pallas kernels: 41.7 us -> 33.5 us
  local copies, waits for them, and re-layouts: 1.87 us -> 0.8 us
    pallas_call x1, Pallas kernels: 41.7 us -> 33.5 us  [shards(): pl.pallas_call(functools.partial(halves_kernel if by_halves else kernel,...]
    unnamed x1, local copies, waits for them, and re-layouts: 1.87 us -> 0.8 us
where the time goes in v2:
time: 34.6 us; the launch traced here: 34.4 us
  Pallas kernels  33.5 us (97%)
  local copies, waits for them, and re-layouts  0.8 us (2%)
    pallas_call x1, Pallas kernels, shards(): pl.pallas_call(functools.partial(halves_kernel if by_halves else kernel,...  33.5 us
    unnamed x1, local copies, waits for them, and re-layouts  0.8 us

profile of v2, /device:TPU:0, one launch (start us, length us, event | category | flops | bytes accessed | tf_op | source)
XLA Modules:
  0.0 34.4 jit_solution(18101016228844176917)
XLA Ops:
  0.0 33.5 %shard_map.82 = bf16[4,256,256]{2,1,0:T(8,128)(2,1)S(1)} custom-call(s32[16]{0:T(128)} %bitcast.9, s32[8]{0:T(128)} %place.1, s32[8]{0:T(128)} %left_sizes.1, s32[8]{0:T(128)} %right_sizes.1, bf16[2,16,16]{2,1,0:T(8,128)(2,1)} %ops_ref.1, bf16[16,256,256]{2,1,0:T(8,128)(2,1)} %bitcast.6, bf16[2,256,256]{2,1,0:T(8,128)(2,1)} %bitcast.7, ...), custom_call_target="tpu_custom_call" | custom-call | tf_op jit(solution)/shard_map/pallas_call | solution.py:803
  33.6 0.8 %copy.10 = bf16[1,4,256,256]{3,2,1,0:T(8,128)(2,1)} copy(bf16[1,4,256,256]{3,2,1,0:T(8,128)(2,1)S(1)} %bitcast.5) | data formatting | bytes 1048576

commit v3 on v2

--- a/solution.py
+++ b/solution.py
@@ -422,6 +422,17 @@
     def own_half(h, of):
         return right_hbm.at[h, pl.ds(pl.multiple_of(of * half, half), half)]
 
+    barrier = pltpu.get_barrier_semaphore()
+    for target in (L, X):
+        pl.semaphore_signal(barrier, inc=1, device_id=(targets[target], p), device_id_type=MESH)
+
+    @pl.when(jnp.logical_not(end))
+    def _():
+        pl.semaphore_signal(barrier, inc=1, device_id=(targets[S], p), device_id_type=MESH)
+
+    for other in (sibling, peer):
+        pl.semaphore_signal(barrier, inc=1, device_id=(b, other), device_id_type=MESH)
+
     wave_copy = pltpu.make_async_copy(wave_hbm, wave, local_sem.at[0])
     left_copy = pltpu.make_async_copy(left_hbm, left.at[pl.ds(0, channels)], local_sem.at[1])
     own_copies = [
@@ -434,18 +445,6 @@
     for own in own_copies:
         own.start()
     left_copy.start()
-    wave_copy.start()
-
-    barrier = pltpu.get_barrier_semaphore()
-    for target in (L, X):
-        pl.semaphore_signal(barrier, inc=1, device_id=(targets[target], p), device_id_type=MESH)
-
-    @pl.when(jnp.logical_not(end))
-    def _():
-        pl.semaphore_signal(barrier, inc=1, device_id=(targets[S], p), device_id_type=MESH)
-
-    for other in (sibling, peer):
-        pl.semaphore_signal(barrier, inc=1, device_id=(b, other), device_id_type=MESH)
     pl.semaphore_wait(barrier, 5 - end.astype(jnp.int32))
 
     def to_device(src, dst, send, recv, device):
@@ -600,6 +599,7 @@
                 coef[u, i] = jnp.broadcast_to(column, (states, 128))
 
     ops[pl.ds(0, channels)] = ops_ref[...]
+    wave_copy.start()
     run("own")
     pick_operators()
     run("start")

time: 34.6 us -> 34.6 us (level)
  no operation moved by 1% of the time
where the time goes in v3:
time: 34.6 us; the launch traced here: 34.3 us
  Pallas kernels  33.5 us (97%)
  local copies, waits for them, and re-layouts  0.8 us (2%)
    pallas_call x1, Pallas kernels, shards(): pl.pallas_call(functools.partial(halves_kernel if by_halves else kernel,...  33.5 us
    unnamed x1, local copies, waits for them, and re-layouts  0.8 us

profile of v3, /device:TPU:0, one launch (start us, length us, event | category | flops | bytes accessed | tf_op | source)
XLA Modules:
  0.0 34.3 jit_solution(7473558973541013309)
XLA Ops:
  0.0 33.5 %shard_map.82 = bf16[4,256,256]{2,1,0:T(8,128)(2,1)S(1)} custom-call(s32[16]{0:T(128)} %bitcast.9, s32[8]{0:T(128)} %place.1, s32[8]{0:T(128)} %left_sizes.1, s32[8]{0:T(128)} %right_sizes.1, bf16[2,16,16]{2,1,0:T(8,128)(2,1)} %ops_ref.1, bf16[16,256,256]{2,1,0:T(8,128)(2,1)} %bitcast.6, bf16[2,256,256]{2,1,0:T(8,128)(2,1)} %bitcast.7, ...), custom_call_target="tpu_custom_call" | custom-call | tf_op jit(solution)/shard_map/pallas_call | solution.py:803
  33.6 0.8 %copy.10 = bf16[1,4,256,256]{3,2,1,0:T(8,128)(2,1)} copy(bf16[1,4,256,256]{3,2,1,0:T(8,128)(2,1)S(1)} %bitcast.5) | data formatting | bytes 1048576

commit v4 on v3

--- a/solution.py
+++ b/solution.py
@@ -687,35 +687,53 @@
         def _():
             settled(right_all.at[pl.ds(0, 3)], gather_send.at[0])
 
+    def on_core(core, *jobs):
+        @pl.when(c == core)
+        def _():
+            for job, k in jobs:
+                job(k)
+
     def step(k, _):
+        @pl.when(k == 7)
+        def _():
+            on_core(0, (add_up, 6), (pass_on, 2), (pass_on, 3))
+            on_core(1, (pass_on, 0), (pass_on, 1))
+            free_sends()
+
         for stage in range(1, n):
             @pl.when(k == stage)
             def _():
-                if stage == 7:
-                    add_up(6)
-                    pass_on(3)
-                    pass_on(4)
-                    free_sends()
                 run(stage)
                 if stage == 5:
-                    add_up(4)
-                    pass_on(1)
+                    on_core(0, (add_up, 4), (pass_on, 1))
+                    on_core(1, (add_up, 2), (add_up, 3))
                     run("5+")
 
         compute(k)
 
-        @pl.when((k >= 1) & (k != 5) & (k != 7))
+        @pl.when((c == 0) & (k >= 1) & (k != 5) & (k != 7))
         def _():
             add_up(k - 1)
 
-        @pl.when((k == 4) | (k == 6))
-        def _():
-            pass_on(k - 4)
+        @pl.when((c == 1) & ((k == 3) | (k == 4)))
+        def _():
+            add_up(k - 3)
+
+        @pl.when(k == 4)
+        def _():
+            on_core(0, (pass_on, 0))
+
+        @pl.when(k == 6)
+        def _():
+            on_core(1, (add_up, 4))
 
         return 0
 
     lax.fori_loop(0, n, step, 0)
+    on_core(1, (add_up, 5), (add_up, 6))
     add_up(7)
+    on_core(1, (pass_on, 2), (pass_on, 3))
+    pass_on(4)
     pass_on(5)
     pass_on(6)
 

time: 34.6 us -> 35.1 us (1.014)
  Pallas kernels: 33.5 us -> 34.1 us
    pallas_call x1, Pallas kernels: 33.5 us -> 34.1 us  [shards(): pl.pallas_call(functools.partial(halves_kernel if by_halves else kernel,...]
where the time goes in v4:
time: 35.1 us; the launch traced here: 34.9 us
  Pallas kernels  34.1 us (97%)
  local copies, waits for them, and re-layouts  0.8 us (2%)
    pallas_call x1, Pallas kernels, shards(): pl.pallas_call(functools.partial(halves_kernel if by_halves else kernel,...  34.1 us
    unnamed x1, local copies, waits for them, and re-layouts  0.8 us

profile of v4, /device:TPU:0, one launch (start us, length us, event | category | flops | bytes accessed | tf_op | source)
XLA Modules:
  0.0 34.9 jit_solution(4871323520303878533)
XLA Ops:
  0.0 34.1 %shard_map.82 = bf16[4,256,256]{2,1,0:T(8,128)(2,1)S(1)} custom-call(s32[16]{0:T(128)} %bitcast.9, s32[8]{0:T(128)} %place.1, s32[8]{0:T(128)} %left_sizes.1, s32[8]{0:T(128)} %right_sizes.1, bf16[2,16,16]{2,1,0:T(8,128)(2,1)} %ops_ref.1, bf16[16,256,256]{2,1,0:T(8,128)(2,1)} %bitcast.6, bf16[2,256,256]{2,1,0:T(8,128)(2,1)} %bitcast.7, ...), custom_call_target="tpu_custom_call" | custom-call | tf_op jit(solution)/shard_map/pallas_call | solution.py:821
  34.1 0.8 %copy.10 = bf16[1,4,256,256]{3,2,1,0:T(8,128)(2,1)} copy(bf16[1,4,256,256]{3,2,1,0:T(8,128)(2,1)S(1)} %bitcast.5) | data formatting | bytes 1048576

commit v5 on v4

--- a/solution.py
+++ b/solution.py
@@ -397,9 +397,9 @@
     sector, place, left_sizes, right_sizes, ops_ref,
     wave_hbm, left_hbm, right_hbm,
     out_ref,
-    right_all, away, wave, left, ops, coef, part, part_out, part_in, fin, arr, states_of, mine,
+    right_all, away, wave, left, ops, coef, part, part_out, part_in, fin, arr, states_of, mine, held,
     local_sem, gather_send, gather_recv, early_send, left_recv, ops_send, ops_recv,
-    part_send, part_recv, fin_send, fin_recv, pass_send, pass_recv,
+    part_send, part_recv, fin_send, fin_recv, pass_send, pass_recv, piece_recv,
 ):
     nz, nx = plane_of(n)
     states, rows, _ = wave.shape
@@ -459,11 +459,17 @@
             (targets[kind], p),
         )
 
-    def first(h):
+    whole = pl.ds(0, half)
+    pieces = (pl.ds(0, half // 2), pl.ds(half // 2, half // 2))
+
+    def first(h, at, recv):
         return to_device(
-            away.at[h], right_all.at[b, channels + h], early_send,
-            gather_recv.at[b, channels + h], (b, peer),
-        )
+            away.at[h, at], right_all.at[b, channels + h, at], early_send, recv, (b, peer)
+        )
+
+    firsts = [(0, pieces[0], piece_recv), (0, pieces[1], gather_recv.at[b, channels])] + [
+        (h, whole, gather_recv.at[b, channels + h]) for h in range(1, channels)
+    ]
 
     def left_to_peer(h):
         return to_device(
@@ -475,8 +481,9 @@
     )
 
     pltpu.make_async_copy(right_hbm, left.at[pl.ds(0, channels)], local_sem.at[2]).wait()
+    for h, at, recv in firsts:
+        first(h, at, recv).start()
     for h in range(channels):
-        first(h).start()
         for kind in (L, X):
             hop(b, h, kind, right_all.at[b, h], 0).start()
 
@@ -494,6 +501,15 @@
 
     def event(off, other, u, kinds):
         pos = place_of(off, other)
+        if (off, other, u) == (0, 0, channels):
+            for first_of in firsts[:2]:
+                first(*first_of).wait_recv()
+                view = right_all.at[b, u, first_of[1]]
+                for kind in kinds:
+                    to_device(
+                        view, view, gather_send.at[0], gather_recv.at[b, u], (targets[kind], p)
+                    ).start()
+            return
         hop(pos, u, X, right_all.at[pos, u]).wait_recv()
         for kind in kinds:
             hop(pos, u, kind, right_all.at[pos, u], 0 if (off, other) == (0, 0) else 1).start()
@@ -513,9 +529,9 @@
         3: [(2, 0, 3, (X,))] + [(1, 1, u, ()) for u in range(units)],
         4: [(3, 0, 0, (X,))],
         5: [(3, 0, 1, (X,))],
-        "5+": [(2, 1, u, ()) for u in range(units)],
-        6: [(3, 0, u, ()) for u in hi],
-        7: [(3, 1, u, ()) for u in range(units)],
+        "5 low": [(2, 1, u, ()) for u in lo],
+        "5 high": [(2, 1, u, ()) for u in hi],
+        "6 high": [(3, 0, u, ()) for u in hi],
     }
     mid_before = {
         "own": [
@@ -530,9 +546,11 @@
         3: [(2, 0, 3, (S,))],
         4: [(2, 1, 2, (S,))] + [(-1, 1, u, ()) for u in lo],
         5: [(2, 1, 3, (S,))],
-        6: [(1, 1, u, ()) for u in range(units)],
-        7: [(2, 1, u, ()) for u in lo],
+        "6 low": [(1, 1, u, ()) for u in lo],
+        "6 high": [(1, 1, u, ()) for u in hi],
     }
+
+    last_mid = lo
 
     def run(stage):
         @pl.when(end)
@@ -619,45 +637,86 @@
         )
 
     def to_peer(pos):
-        return to_device(
-            fin.at[pos, c], arr.at[pos, c], fin_send, fin_recv.at[pos], (b, peer)
-        )
-
-    def passing(pos, rank):
-        return to_device(
-            arr.at[pos, rank], arr.at[pos, rank], pass_send, pass_recv, (b, sibling)
-        )
-
-    def compute(k):
-        pos = pos_of(k)
-        s1, s2 = states_of[k, 0], states_of[k, 1]
+        return to_device(fin.at[pos], arr.at[pos], fin_send, fin_recv.at[pos], (b, peer))
+
+    def passing(pos):
+        return to_device(arr.at[pos], arr.at[pos], pass_send, pass_recv, (b, sibling))
+
+    def masked_pair(k):
         live = (row_index < left_sizes[b]) & (column_index < states_of[k, 2])
 
         def masked(s):
             return jnp.where(live, wave[s].astype(f32), 0.0).astype(bf16)
 
-        both = jnp.concatenate([masked(s1), masked(s2)], axis=0)
+        return jnp.concatenate([masked(states_of[k, 0]), masked(states_of[k, 1])], axis=0)
+
+    def products(k, both, units_of, factor):
+        parts = lax.dot_general(
+            both, factor, (((1,), (1,)), ((), ())), preferred_element_type=f32
+        ).astype(bf16).astype(f32)
         total = None
-        for g in range(2):
-            factor = right_all[pos, pl.ds(g * channels, channels)].reshape(channels * half, rows)
-            parts = lax.dot_general(
-                both, factor, (((1,), (1,)), ((), ())), preferred_element_type=f32
-            ).astype(bf16).astype(f32)
-            for h in range(channels):
-                u = g * channels + h
-                p1 = parts[:rows, h * half:(h + 1) * half]
-                p2 = parts[rows:, h * half:(h + 1) * half]
-                own1, own2 = coef[u, 0, pl.ds(2 * k, 1)], coef[u, 0, pl.ds(2 * k + 1, 1)]
-                cross1, cross2 = coef[u, 1, pl.ds(2 * k, 1)], coef[u, 1, pl.ds(2 * k + 1, 1)]
-                mixed = jnp.concatenate(
-                    [(own1 * p1 + cross1 * p2).astype(bf16), (cross2 * p1 + own2 * p2).astype(bf16)],
-                    axis=1,
-                )
-                product = jnp.dot(left[u], mixed, preferred_element_type=f32)
-                total = product if total is None else total + product
+        for i, u in enumerate(units_of):
+            p1 = parts[:rows, i * half:(i + 1) * half]
+            p2 = parts[rows:, i * half:(i + 1) * half]
+            own1, own2 = coef[u, 0, pl.ds(2 * k, 1)], coef[u, 0, pl.ds(2 * k + 1, 1)]
+            cross1, cross2 = coef[u, 1, pl.ds(2 * k, 1)], coef[u, 1, pl.ds(2 * k + 1, 1)]
+            mixed = jnp.concatenate(
+                [(own1 * p1 + cross1 * p2).astype(bf16), (cross2 * p1 + own2 * p2).astype(bf16)],
+                axis=1,
+            )
+            product = jnp.dot(left[u], mixed, preferred_element_type=f32)
+            total = product if total is None else total + product
+        return total
+
+    def some(k, both, units_of):
+        factor = right_all[pos_of(k), pl.ds(units_of[0], channels)].reshape(channels * half, rows)
+        return products(k, both, units_of, factor)
+
+    def give(k, total):
+        pos = pos_of(k)
         part_out[pos] = total.astype(bf16)
         to_sibling(pos).start()
-        part[pos] = total
+
+    def compute(k):
+        both = masked_pair(k)
+        total = some(k, both, lo) + some(k, both, hi)
+        give(k, total)
+        part[pos_of(k)] = total
+
+    def finish(k, total):
+        part[pos_of(k)] = total
+
+        @pl.when(c == 0)
+        def _():
+            add_up(k)
+            send(k)
+
+        give(k, part[pos_of(k)])
+
+    def compute_last(k):
+        pos = pos_of(k)
+        held[...] = masked_pair(k)
+        for i in range(channels):
+            pair = (i, channels + i)
+
+            @pl.when(end)
+            def _():
+                for u in pair:
+                    event(3, 1, u, ())
+
+            @pl.when(jnp.logical_not(end))
+            def _():
+                if pair[0] in last_mid:
+                    event(2, 1, pair[0], ())
+
+            factor = jnp.concatenate([right_all[pos, u] for u in pair], axis=0)
+            total = products(k, held[...], pair, factor)
+            if i == 0:
+                part[pos] = total
+            elif i < channels - 1:
+                part[pos] += total
+            else:
+                finish(k, part[pos] + total)
 
     def add_up(k):
         pos = pos_of(k)
@@ -667,12 +726,14 @@
             cut = slice(r * half, (r + 1) * half)
             total = part[pos, :, cut] + part_in[pos, :, cut].astype(f32)
             fin[pos, r] = jnp.where(live, total, 0.0).astype(bf16)
-        to_peer(pos).start()
+
+    def send(k):
+        to_peer(pos_of(k)).start()
 
     def pass_on(k):
         pos = pos_of(k)
         to_peer(pos).wait_recv()
-        passing(pos, c).start()
+        passing(pos).start()
 
     def free_sends():
         settled(left.at[pl.ds(0, channels + channels // 2)], early_send)
@@ -694,66 +755,84 @@
                 job(k)
 
     def step(k, _):
-        @pl.when(k == 7)
-        def _():
-            on_core(0, (add_up, 6), (pass_on, 2), (pass_on, 3))
-            on_core(1, (pass_on, 0), (pass_on, 1))
-            free_sends()
-
-        for stage in range(1, n):
+        for stage in range(1, 5):
             @pl.when(k == stage)
             def _():
                 run(stage)
-                if stage == 5:
-                    on_core(0, (add_up, 4), (pass_on, 1))
-                    on_core(1, (add_up, 2), (add_up, 3))
-                    run("5+")
 
         compute(k)
 
-        @pl.when((c == 0) & (k >= 1) & (k != 5) & (k != 7))
+        @pl.when((c == 0) & (k >= 1))
         def _():
             add_up(k - 1)
-
-        @pl.when((c == 1) & ((k == 3) | (k == 4)))
+            send(k - 1)
+
+        @pl.when((c == 1) & (k >= 3))
         def _():
             add_up(k - 3)
 
-        @pl.when(k == 4)
-        def _():
-            on_core(0, (pass_on, 0))
-
-        @pl.when(k == 6)
-        def _():
-            on_core(1, (add_up, 4))
-
         return 0
 
-    lax.fori_loop(0, n, step, 0)
-    on_core(1, (add_up, 5), (add_up, 6))
-    add_up(7)
-    on_core(1, (pass_on, 2), (pass_on, 3))
-    pass_on(4)
-    pass_on(5)
-    pass_on(6)
+    def low_half(k, _):
+        for stage in (5, 6):
+            @pl.when(k == stage)
+            def _():
+                run(f"{stage} low")
+
+        part[pos_of(k)] = some(k, masked_pair(k), lo)
+        return 0
+
+    def high_half(k, _):
+        for stage in (5, 6):
+            @pl.when(k == stage)
+            def _():
+                run(f"{stage} high")
+
+        finish(k, part[pos_of(k)] + some(k, masked_pair(k), hi))
+
+        @pl.when(c == 1)
+        def _():
+            add_up(k - 3)
+
+        return 0
+
+    lax.fori_loop(0, 5, step, 0)
+    run(5)
+    on_core(0, (add_up, 4), (send, 4))
+    lax.fori_loop(5, 7, low_half, 0)
+    lax.fori_loop(5, 7, high_half, 0)
+    on_core(0, (pass_on, 0), (pass_on, 1), (pass_on, 2))
+    free_sends()
+    compute_last(7)
+    on_core(1, (add_up, 4))
+    on_core(0, *[(pass_on, k) for k in range(3, n - 1)])
+    on_core(1, (add_up, 5), (add_up, 6), (add_up, 7))
 
     @pl.when(jnp.logical_not(end))
     def _():
         settled(right_all.at[pl.ds(0, 6)], gather_send.at[1])
 
     settled(part_out, part_send)
-    settled(arr.at[pl.ds(0, n // 2)], fin_send)
-    pass_on(7)
-    passed = arr.at[pl.ds(0, n // 2)]
-    to_device(passed, passed, pass_send, pass_recv, (b, sibling)).wait_recv()
     mine_at = pl.ds(pl.multiple_of(y * half, half), half)
     others_at = pl.ds(pl.multiple_of((1 - y) * half, half), half)
     for q in range(per):
-        pos, rank = mine[q, 0], mine[q, 1]
-        out_ref[q, :, mine_at] = fin[pos, rank]
-        out_ref[q, :, others_at] = arr[pos, rank]
-
-    settled(arr.at[pl.ds(0, n // 2)], pass_send)
+        out_ref[q, :, mine_at] = fin[mine[q, 0], mine[q, 1]]
+
+    @pl.when(c == 0)
+    def _():
+        settled(arr, fin_send)
+        pass_on(n - 1)
+
+    @pl.when(c == 1)
+    def _():
+        to_device(arr, arr, pass_send, pass_recv, (b, sibling)).wait_recv()
+
+    for q in range(per):
+        out_ref[q, :, others_at] = arr[mine[q, 0], mine[q, 1]]
+
+    @pl.when(c == 0)
+    def _():
+        settled(arr, pass_send)
 
 
 def shards(n, m, wave_blocks, left_environment, right_environment, site_operators,
@@ -789,8 +868,9 @@
             pltpu.VMEM((n, 2) + tall, bf16),
             pltpu.SMEM((n, 3), jnp.int32),
             pltpu.SMEM((per, 2), jnp.int32),
+            pltpu.VMEM((2 * rows, rows), bf16),
             dma((3,)), dma((2,)), dma((n, 2 * channels)), dma, dma, dma, dma,
-            dma, dma((n,)), dma, dma((n,)), dma, dma,
+            dma, dma((n,)), dma, dma((n,)), dma, dma, dma,
         ]
     elif ny == 2 and cores == 2:
         rest = [

time: 35.1 us -> 34.4 us (0.980)
  Pallas kernels: 34.1 us -> 33.4 us
    pallas_call x1, Pallas kernels: 34.1 us -> 33.4 us  [shards(): pl.pallas_call(functools.partial(halves_kernel if by_halves else kernel,...]
where the time goes in v5:
time: 34.4 us; the launch traced here: 34.2 us
  Pallas kernels  33.4 us (97%)
  local copies, waits for them, and re-layouts  0.8 us (2%)
    pallas_call x1, Pallas kernels, shards(): pl.pallas_call(functools.partial(halves_kernel if by_halves else kernel,...  33.4 us
    unnamed x1, local copies, waits for them, and re-layouts  0.8 us

profile of v5, /device:TPU:0, one launch (start us, length us, event | category | flops | bytes accessed | tf_op | source)
XLA Modules:
  0.0 34.2 jit_solution(5372862083866715277)
XLA Ops:
  0.0 33.4 %shard_map.82 = bf16[4,256,256]{2,1,0:T(8,128)(2,1)S(1)} custom-call(s32[16]{0:T(128)} %bitcast.9, s32[8]{0:T(128)} %place.1, s32[8]{0:T(128)} %left_sizes.1, s32[8]{0:T(128)} %right_sizes.1, bf16[2,16,16]{2,1,0:T(8,128)(2,1)} %ops_ref.1, bf16[16,256,256]{2,1,0:T(8,128)(2,1)} %bitcast.6, bf16[2,256,256]{2,1,0:T(8,128)(2,1)} %bitcast.7, ...), custom_call_target="tpu_custom_call" | custom-call | tf_op jit(solution)/shard_map/pallas_call | solution.py:901
  33.4 0.8 %copy.10 = bf16[1,4,256,256]{3,2,1,0:T(8,128)(2,1)} copy(bf16[1,4,256,256]{3,2,1,0:T(8,128)(2,1)S(1)} %bitcast.5) | data formatting | bytes 1048576

commit v6 on v5

--- a/solution.py
+++ b/solution.py
@@ -493,8 +493,11 @@
 
     left_copy.wait()
     ops_to_peer.start()
-    for h in range(channels):
-        left_to_peer(h).start()
+
+    def send_left():
+        for h in range(channels):
+            left_to_peer(h).start()
+
 
     def place_of(off, other):
         return (z + way * off) * nx + ((1 - x) if other else x)
@@ -619,6 +622,7 @@
     ops[pl.ds(0, channels)] = ops_ref[...]
     wave_copy.start()
     run("own")
+    send_left()
     pick_operators()
     run("start")
 
@@ -758,6 +762,8 @@
         for stage in range(1, 5):
             @pl.when(k == stage)
             def _():
+                if stage >= 2:
+                    on_core(1, (add_up, stage - 2))
                 run(stage)
 
         compute(k)
@@ -766,10 +772,6 @@
         def _():
             add_up(k - 1)
             send(k - 1)
-
-        @pl.when((c == 1) & (k >= 3))
-        def _():
-            add_up(k - 3)
 
         return 0
 
@@ -789,14 +791,10 @@
                 run(f"{stage} high")
 
         finish(k, part[pos_of(k)] + some(k, masked_pair(k), hi))
-
-        @pl.when(c == 1)
-        def _():
-            add_up(k - 3)
-
         return 0
 
     lax.fori_loop(0, 5, step, 0)
+    on_core(1, (add_up, 3))
     run(5)
     on_core(0, (add_up, 4), (send, 4))
     lax.fori_loop(5, 7, low_half, 0)

time: 34.4 us -> 33.7 us (0.980)
  Pallas kernels: 33.4 us -> 32.7 us
    pallas_call x1, Pallas kernels: 33.4 us -> 32.7 us  [shards(): pl.pallas_call(functools.partial(halves_kernel if by_halves else kernel,...]
where the time goes in v6:
time: 33.7 us; the launch traced here: 33.5 us
  Pallas kernels  32.7 us (97%)
  local copies, waits for them, and re-layouts  0.8 us (2%)
    pallas_call x1, Pallas kernels, shards(): pl.pallas_call(functools.partial(halves_kernel if by_halves else kernel,...  32.7 us
    unnamed x1, local copies, waits for them, and re-layouts  0.8 us

profile of v6, /device:TPU:0, one launch (start us, length us, event | category | flops | bytes accessed | tf_op | source)
XLA Modules:
  0.0 33.5 jit_solution(8067382924739567123)
XLA Ops:
  0.0 32.7 %shard_map.82 = bf16[4,256,256]{2,1,0:T(8,128)(2,1)S(1)} custom-call(s32[16]{0:T(128)} %bitcast.9, s32[8]{0:T(128)} %place.1, s32[8]{0:T(128)} %left_sizes.1, s32[8]{0:T(128)} %right_sizes.1, bf16[2,16,16]{2,1,0:T(8,128)(2,1)} %ops_ref.1, bf16[16,256,256]{2,1,0:T(8,128)(2,1)} %bitcast.6, bf16[2,256,256]{2,1,0:T(8,128)(2,1)} %bitcast.7, ...), custom_call_target="tpu_custom_call" | custom-call | tf_op jit(solution)/shard_map/pallas_call | solution.py:899
  32.7 0.8 %copy.10 = bf16[1,4,256,256]{3,2,1,0:T(8,128)(2,1)} copy(bf16[1,4,256,256]{3,2,1,0:T(8,128)(2,1)S(1)} %bitcast.5) | data formatting | bytes 1048576

commit v7 on v6

--- a/solution.py
+++ b/solution.py
@@ -399,7 +399,7 @@
     out_ref,
     right_all, away, wave, left, ops, coef, part, part_out, part_in, fin, arr, states_of, mine, held,
     local_sem, gather_send, gather_recv, early_send, left_recv, ops_send, ops_recv,
-    part_send, part_recv, fin_send, fin_recv, pass_send, pass_recv, piece_recv,
+    part_send, part_recv, fin_send, fin_recv, pass_send, pass_recv, piece_recv, last_recv,
 ):
     nz, nx = plane_of(n)
     states, rows, _ = wave.shape
@@ -533,7 +533,8 @@
         4: [(3, 0, 0, (X,))],
         5: [(3, 0, 1, (X,))],
         "5 low": [(2, 1, u, ()) for u in lo],
-        "5 high": [(2, 1, u, ()) for u in hi],
+        "5 third": [(2, 1, channels, ())],
+        "5 last": [(2, 1, u, ()) for u in hi[1:]],
         "6 high": [(3, 0, u, ()) for u in hi],
     }
     mid_before = {
@@ -643,6 +644,13 @@
     def to_peer(pos):
         return to_device(fin.at[pos], arr.at[pos], fin_send, fin_recv.at[pos], (b, peer))
 
+    def rank_to_peer(pos, r):
+        recv = fin_recv.at[pos] if r == 0 else last_recv
+        return to_device(fin.at[pos, r], arr.at[pos, r], fin_send, recv, (b, peer))
+
+    def rank_passing(pos, r):
+        return to_device(arr.at[pos, r], arr.at[pos, r], pass_send, pass_recv, (b, sibling))
+
     def passing(pos):
         return to_device(arr.at[pos], arr.at[pos], pass_send, pass_recv, (b, sibling))
 
@@ -699,7 +707,6 @@
 
     def compute_last(k):
         pos = pos_of(k)
-        held[...] = masked_pair(k)
         for i in range(channels):
             pair = (i, channels + i)
 
@@ -714,7 +721,7 @@
                     event(2, 1, pair[0], ())
 
             factor = jnp.concatenate([right_all[pos, u] for u in pair], axis=0)
-            total = products(k, held[...], pair, factor)
+            total = products(k, held[k - 5], pair, factor)
             if i == 0:
                 part[pos] = total
             elif i < channels - 1:
@@ -732,7 +739,11 @@
             fin[pos, r] = jnp.where(live, total, 0.0).astype(bf16)
 
     def send(k):
-        to_peer(pos_of(k)).start()
+        if isinstance(k, int) and k == n - 1:
+            for r in range(2):
+                rank_to_peer(pos_of(k), r).start()
+        else:
+            to_peer(pos_of(k)).start()
 
     def pass_on(k):
         pos = pos_of(k)
@@ -781,24 +792,32 @@
             def _():
                 run(f"{stage} low")
 
-        part[pos_of(k)] = some(k, masked_pair(k), lo)
+        both = masked_pair(k)
+        held[k - 5] = both
+        part[pos_of(k)] = some(k, both, lo)
         return 0
 
-    def high_half(k, _):
-        for stage in (5, 6):
-            @pl.when(k == stage)
-            def _():
-                run(f"{stage} high")
-
-        finish(k, part[pos_of(k)] + some(k, masked_pair(k), hi))
-        return 0
+    def one(k, u):
+        return products(k, held[k - 5], (u,), right_all[pos_of(k), u])
+
+    def high_half(k):
+        run(f"{k} high")
+        finish(k, part[pos_of(k)] + some(k, held[k - 5], hi))
 
     lax.fori_loop(0, 5, step, 0)
     on_core(1, (add_up, 3))
     run(5)
     on_core(0, (add_up, 4), (send, 4))
     lax.fori_loop(5, 7, low_half, 0)
-    lax.fori_loop(5, 7, high_half, 0)
+    held[2] = masked_pair(7)
+    run("5 third")
+    part[pos_of(5)] += one(5, hi[0])
+    run("5 last")
+    total = part[pos_of(5)]
+    for u in hi[1:]:
+        total = total + one(5, u)
+    finish(5, total)
+    high_half(6)
     on_core(0, (pass_on, 0), (pass_on, 1), (pass_on, 2))
     free_sends()
     compute_last(7)
@@ -818,8 +837,10 @@
 
     @pl.when(c == 0)
     def _():
+        for r in range(2):
+            rank_to_peer(pos_of(n - 1), r).wait_recv()
+            rank_passing(pos_of(n - 1), r).start()
         settled(arr, fin_send)
-        pass_on(n - 1)
 
     @pl.when(c == 1)
     def _():
@@ -866,9 +887,9 @@
             pltpu.VMEM((n, 2) + tall, bf16),
             pltpu.SMEM((n, 3), jnp.int32),
             pltpu.SMEM((per, 2), jnp.int32),
-            pltpu.VMEM((2 * rows, rows), bf16),
+            pltpu.VMEM((3, 2 * rows, rows), bf16),
             dma((3,)), dma((2,)), dma((n, 2 * channels)), dma, dma, dma, dma,
-            dma, dma((n,)), dma, dma((n,)), dma, dma, dma,
+            dma, dma((n,)), dma, dma((n,)), dma, dma, dma, dma,
         ]
     elif ny == 2 and cores == 2:
         rest = [

time: 33.7 us -> 33.5 us (level)
  no operation moved by 1% of the time
where the time goes in v7:
time: 33.5 us; the launch traced here: 33.3 us
  Pallas kernels  32.5 us (97%)
  local copies, waits for them, and re-layouts  0.8 us (2%)
    pallas_call x1, Pallas kernels, shards(): pl.pallas_call(functools.partial(halves_kernel if by_halves else kernel,...  32.5 us
    unnamed x1, local copies, waits for them, and re-layouts  0.8 us

profile of v7, /device:TPU:0, one launch (start us, length us, event | category | flops | bytes accessed | tf_op | source)
XLA Modules:
  0.0 33.3 jit_solution(4692540786551941609)
XLA Ops:
  0.0 32.5 %shard_map.82 = bf16[4,256,256]{2,1,0:T(8,128)(2,1)S(1)} custom-call(s32[16]{0:T(128)} %bitcast.9, s32[8]{0:T(128)} %place.1, s32[8]{0:T(128)} %left_sizes.1, s32[8]{0:T(128)} %right_sizes.1, bf16[2,16,16]{2,1,0:T(8,128)(2,1)} %ops_ref.1, bf16[16,256,256]{2,1,0:T(8,128)(2,1)} %bitcast.6, bf16[2,256,256]{2,1,0:T(8,128)(2,1)} %bitcast.7, ...), custom_call_target="tpu_custom_call" | custom-call | tf_op jit(solution)/shard_map/pallas_call | solution.py:920
  32.5 0.8 %copy.10 = bf16[1,4,256,256]{3,2,1,0:T(8,128)(2,1)} copy(bf16[1,4,256,256]{3,2,1,0:T(8,128)(2,1)S(1)} %bitcast.5) | data formatting | bytes 1048576
